TPU v7x, 128 devices: a whole 4x4x4 slice. The times are simulated.
128 devices in a mesh: req: 8 (over x, core), mlp: 16 (over z, y).
Axes of the slice: x: 4, y: 4, z: 4, core: 2. Of those that a mesh axis runs over, the one named last changes fastest.
Arguments:
- tokens: bfloat16 [8192, 4096], P(('req', 'mlp')), may hold values from -6 to 6
- layer_norm_gain: float32 [4096], replicated, may hold values from 0.1 to 1.9
- layer_norm_bias: float32 [4096], replicated, may hold values from -2 to 2
- query_key_weight: bfloat16 [4096, 16, 768], P(None, 'mlp')
- output_weight: bfloat16 [16, 256, 4096], P('mlp'), may hold values from -0.09375 to 0.09375
- up_weight: bfloat16 [4096, 8192], P(None, 'mlp'), may hold values from -0.09375 to 0.09375
- input_bias: float32 [8192], P('mlp'), may hold values from -3 to 3
- down_weight: bfloat16 [8192, 4096], P('mlp'), may hold values from -0.0625 to 0.0625
- output_bias: float32 [4096], replicated, may hold values from -2 to 2
- input_adapter_left: bfloat16 [4096, 2048], P(None, 'mlp'), may hold values from -0.09375 to 0.09375
- query_key_value_right: bfloat16 [1024, 16, 768], P(None, 'mlp'), may hold values from -1.5 to 1.5
- up_adapter_right: bfloat16 [1024, 8192], P(None, 'mlp'), may hold values from -1.5 to 1.5
- output_adapter_left: bfloat16 [16, 256, 1024], P('mlp'), may hold values from -0.09375 to 0.09375
- down_adapter_left: bfloat16 [8192, 1024], P('mlp'), may hold values from -0.0625 to 0.0625
- output_adapter_right: bfloat16 [2048, 4096], P('mlp'), may hold values from -1 to 1
- lengths: int32 [257], replicated, may hold values from 8 to 4096, as said below
- request_adapter: int32 [257], replicated, may hold values from 0 to 63
- slot_adapter: int32 [64], P('mlp'), may hold values from 0 to 63, each once
Outputs:
- mixed: bfloat16 [8192, 4096], P(('req', 'mlp'))
Inputs may be any that keep to these rules, and one draw needn't show every extreme that they name: `lengths`: one request holds exactly 4096 tokens, every other one 8 to 24; together they hold 8192 tokens. `slot_adapter`: every adapter id stands in exactly one slot.
All inputs are finite; a program needn't handle non-finite values.
Results may differ from a plain program's by a relative error of at most 0.017.
Values may be sent and summed in bfloat16 or wider, within the bound.
A program may use at most 128 MiB of HBM per device.

v0:
```python
import math
import jax
import jax.numpy as jnp
from jax import lax
from jax.sharding import PartitionSpec as P

HEAD_SIZE = 256
ROT = 64
ADAPTER_RANK = 16
ADP_DEV = 4
EPSILON = 1e-05
NEGATIVE_FILL = -1e30


def rank_product(left_side, right_side):
    return jnp.dot(left_side, right_side, preferred_element_type=jnp.float32)


def normalize(inputs, layer_norm_gain, layer_norm_bias):
    values = inputs.astype(jnp.float32)
    center = values - jnp.mean(values, axis=1, keepdims=True)
    spread = jnp.mean(center * center, axis=1, keepdims=True)
    scaled = center * lax.rsqrt(spread + EPSILON)
    return (scaled * layer_norm_gain + layer_norm_bias).astype(jnp.bfloat16)


def token_info(lengths, request_adapter, first_row, row_count):
    endings = jnp.cumsum(lengths)
    anchors = endings - lengths
    token_index = first_row + lax.iota(jnp.int32, row_count)
    inside = anchors[None, :] <= token_index[:, None]
    request = jnp.sum(inside.astype(jnp.int32), axis=1) - 1
    request_start = jnp.max(jnp.where(inside, anchors[None, :], jnp.zeros((), jnp.int32)), axis=1)
    adapter_id = jnp.take(request_adapter, jnp.maximum(request, 0))
    return (token_index, request, token_index - request_start, adapter_id)


def rotate(matrix, position):
    row_count = matrix.shape[0]
    head_count = matrix.shape[1]
    half_rot = ROT // 2
    frequency = jnp.exp(jnp.arange(half_rot, dtype=jnp.float32) * (-2.0 * math.log(10000.0) / ROT))
    angles = position.astype(jnp.float32)[:, None] * frequency[None, :]
    cosine = jnp.cos(angles)[:, None, :]
    sine_value = jnp.sin(angles)[:, None, :]
    paired_part = matrix[:, :, :ROT].reshape(row_count, head_count, half_rot, 2)
    even_part = paired_part[:, :, :, 0]
    odd_part = paired_part[:, :, :, 1]
    turned = jnp.stack(
        [even_part * cosine - odd_part * sine_value, odd_part * cosine + even_part * sine_value],
        axis=-1,
    )
    return jnp.concatenate([turned.reshape(row_count, head_count, ROT), matrix[:, :, ROT:]], axis=2)


def slot_selector(products, chosen, adapter_id, column_count):
    row_count = products.shape[0]
    selector = (adapter_id[:, None] == chosen[None, :]).astype(jnp.float32)
    reshaped = products.reshape(row_count, chosen.shape[0], column_count)
    return jnp.sum(selector[:, :, None] * reshaped, axis=1)


def widen_rows(values, chosen, adapter_id):
    selector = adapter_id[:, None] == chosen[None, :]
    spread = jnp.where(selector[:, :, None], values[:, None, :], jnp.zeros((), values.dtype))
    return spread.reshape(values.shape[0], chosen.shape[0] * values.shape[1])


def per_device(
    tokens,
    layer_norm_gain,
    layer_norm_bias,
    query_key_weight,
    output_weight,
    up_weight,
    input_bias,
    down_weight,
    output_bias,
    input_adapter_left,
    query_key_value_right,
    up_adapter_right,
    output_adapter_left,
    down_adapter_left,
    output_adapter_right,
    lengths,
    request_adapter,
    slot_adapter,
):
    tok_dev = tokens.shape[0]
    model_width = tokens.shape[1]
    mlp_count = lax.axis_size("mlp")
    tok_grp = tok_dev * mlp_count
    group_first = lax.axis_index("req") * tok_grp
    heads_local = query_key_weight.shape[1]
    hid_local = up_weight.shape[1]
    adapter_ids = slot_adapter.shape[0] * mlp_count
    every_id = lax.iota(jnp.int32, adapter_ids)
    query_key_columns = heads_local * 3 * HEAD_SIZE
    attention_columns = heads_local * HEAD_SIZE
    query_key_rows = query_key_weight.reshape(model_width, query_key_columns)
    normed_rows = normalize(tokens, layer_norm_gain, layer_norm_bias)
    slot_portion = lax.all_gather(normed_rows, "mlp", axis=0, tiled=True)
    grouped = jnp.concatenate(
        [
            rank_product(slot_portion, query_key_rows),
            rank_product(slot_portion, up_weight),
            rank_product(slot_portion, input_adapter_left),
        ],
        axis=1,
    )
    token_index, request, position, adapter_id = token_info(
        lengths, request_adapter, group_first, tok_grp
    )
    rank_part = slot_selector(
        grouped[:, query_key_columns + hid_local :], slot_adapter, adapter_id, 2 * ADAPTER_RANK
    )
    rank_input = lax.psum(rank_part.astype(jnp.bfloat16), "mlp")
    qkv_extra = rank_product(
        widen_rows(rank_input[:, :ADAPTER_RANK], every_id, adapter_id),
        query_key_value_right.reshape(adapter_ids * ADAPTER_RANK, query_key_columns),
    )
    up_delta = rank_product(
        widen_rows(rank_input[:, ADAPTER_RANK:], every_id, adapter_id), up_adapter_right
    )
    projected_rows = (grouped[:, :query_key_columns] + qkv_extra).reshape(
        tok_grp, heads_local, 3 * HEAD_SIZE
    )
    hidden_units = jax.nn.gelu(
        grouped[:, query_key_columns : query_key_columns + hid_local] + up_delta + input_bias,
        approximate=True,
    ).astype(jnp.bfloat16)
    queries = rotate(projected_rows[:, :, :HEAD_SIZE], position).astype(jnp.bfloat16)
    key_rows = (
        rotate(projected_rows[:, :, HEAD_SIZE : 2 * HEAD_SIZE], position)
        .astype(jnp.bfloat16)
        .reshape(tok_grp, attention_columns)
    )
    value_rows = (
        projected_rows[:, :, 2 * HEAD_SIZE :]
        .astype(jnp.bfloat16)
        .reshape(tok_grp, attention_columns)
    )
    paired = jnp.stack([key_rows, value_rows])
    score_scale = HEAD_SIZE ** (-0.5)
    last_row = group_first + tok_grp - 1
    start_state = (
        jnp.full((tok_grp, heads_local), NEGATIVE_FILL, jnp.float32),
        jnp.zeros((tok_grp, heads_local), jnp.float32),
        jnp.zeros((tok_grp, heads_local, HEAD_SIZE), jnp.float32),
    )
    slot_portion = lax.all_gather(paired, "req", axis=1, tiled=True)
    offset = jnp.int32(0)
    amount = slot_portion.shape[1]
    key_index, key_request, key_position, key_adapter = token_info(
        lengths, request_adapter, offset, amount
    )
    useful = jnp.logical_and(offset <= last_row, key_request[amount - 1] >= request[0])

    def attend(current):
        running_top, running_total, running_sum = current
        part_keys = slot_portion[0].reshape(amount, heads_local, HEAD_SIZE)
        part_values = slot_portion[1].reshape(amount, heads_local, HEAD_SIZE)
        scores = (
            jnp.einsum("qhd,khd->qhk", queries, part_keys, preferred_element_type=jnp.float32)
            * score_scale
        )
        allowed = jnp.logical_and(
            key_request[None, :] == request[:, None], key_index[None, :] <= token_index[:, None]
        )[:, None, :]
        masked = jnp.where(allowed, scores, NEGATIVE_FILL)
        new_top = jnp.maximum(running_top, jnp.max(masked, axis=2))
        weights = jnp.where(allowed, jnp.exp(masked - new_top[:, :, None]), 0.0)
        new_total = jnp.sum(weights, axis=2)
        new_sum = jnp.einsum(
            "qhk,khd->qhd",
            weights.astype(jnp.bfloat16),
            part_values,
            preferred_element_type=jnp.float32,
        )
        return (new_top, new_total, new_sum)

    final_state = lax.cond(useful, attend, lambda current: current, start_state)
    attention_output = (
        (final_state[2] / final_state[1][:, :, None])
        .astype(jnp.bfloat16)
        .reshape(tok_grp, attention_columns)
    )
    output_rows = output_weight.reshape(attention_columns, model_width)
    own_ids = lax.axis_index("mlp") * ADP_DEV + lax.iota(jnp.int32, ADP_DEV)
    output_rank_rows = rank_product(
        attention_output, output_adapter_left.reshape(attention_columns, adapter_ids * ADAPTER_RANK)
    )
    down_rank_rows = rank_product(hidden_units, down_adapter_left)
    rank_part_out = jnp.concatenate(
        [
            slot_selector(output_rank_rows, every_id, adapter_id, ADAPTER_RANK),
            slot_selector(down_rank_rows, every_id, adapter_id, ADAPTER_RANK),
        ],
        axis=1,
    )
    rank_output = lax.psum(rank_part_out.astype(jnp.bfloat16), "mlp")
    rank_widened = widen_rows(rank_output, own_ids, adapter_id)
    mixed = lax.psum_scatter(
        (
            rank_product(attention_output, output_rows)
            + (
                rank_product(hidden_units, down_weight)
                + rank_product(rank_widened, output_adapter_right)
            )
        ).astype(jnp.bfloat16),
        "mlp",
        scatter_dimension=0,
        tiled=True,
    ).astype(jnp.float32)
    return (mixed + tokens.astype(jnp.float32) + output_bias).astype(jnp.bfloat16)


def solution(mesh):
    in_specs = (
        P(("req", "mlp"), None),
        P(),
        P(),
        P(None, "mlp", None),
        P("mlp", None, None),
        P(None, "mlp"),
        P("mlp"),
        P("mlp", None),
        P(),
        P(None, "mlp"),
        P(None, "mlp", None),
        P(None, "mlp"),
        P("mlp", None, None),
        P("mlp", None),
        P("mlp", None),
        P(),
        P(),
        P("mlp"),
    )
    out_specs = P(("req", "mlp"), None)
    return jax.shard_map(
        per_device, mesh=mesh, in_specs=in_specs, out_specs=out_specs, check_vma=False
    )
```

profile of v0, /device:TPU:0, one launch (start us, length us, event | category | flops | bytes accessed | tf_op | source)
XLA Modules:
  0.0 493.8 jit_solution(12925493245137740278)
XLA Ops:
  6.5 1.4 convert_reduce_fusion.1
  7.9 1.3 fusion.35
  9.3 2.1 fusion.38
  13.8 6.2 %gather_fusion = s32[1024]{0:T(1024)S(1)} fusion(s32[257]{0:T(512)} %param.36, s32[1024]{0:T(1024)S(1)} %maximum_clamp_fusion), kind=kCustom, calls=%fused_computation | custom fusion | bytes 12288 | tf_op jit(solution)/shard_map/jit(_take)/gather | solution.py:34
  20.8 64.1 %all-gather.3.cloned.1.call-done = bf16[1024,4096]{1,0:T(8,128)(2,1)} async-done(((bf16[64,4096]{1,0:T(8,128)(2,1)}), bf16[1024,4096]{1,0:T(8,128)(2,1)}) %all-gather.3.cloned.1.call-update) | async-done | bytes 8388624 | tf_op jit(solution)/shard_map/all_gather | solution.py:102
  84.9 6.3 %fusion.67 = f32[1024,128]{0,1:T(8,128)S(1)} fusion(bf16[1024,4096]{1,0:T(8,128)(2,1)} %all-gather.3.cloned.1.call-done, bf16[4096,128]{1,0:T(8,128)(2,1)S(1)} %copy-done.2), kind=kOutput, calls=%fused_computation.113 | convolution fusion | flops 1073741824 | bytes 9961472 | tf_op jit(solution)/shard_map/dot_general | solution.py:16
  92.5 80.1 %all-reduce.4.cloned.1.call-done = bf16[1024,32]{0,1:T(8,128)(2,1)} async-done(((bf16[1024,32]{0,1:T(8,128)(2,1)}), bf16[1024,32]{0,1:T(8,128)(2,1)}) %all-reduce.4.cloned.1.call-update) | async-done | bytes 65552 | tf_op jit(solution)/shard_map/psum | solution.py:117
  173.4 1.8 broadcast_select_fusion
  175.2 3.3 fusion.29
  178.5 11.0 %fusion.66 = (bf16[1024,1,768]{0,2,1:T(8,128)(2,1)S(1)}, f32[1024,1,768]{0,2,1:T(8,128)S(1)}) fusion(f32[1024,768]{0,1:T(8,128)S(1)} %fusion.29, bf16[1024,4096]{1,0:T(8,128)(2,1)} %all-gather.3.cloned.1.call-done, bf16[4096,1,768]{2,0,1:T(8,128)(2,1)} %param.23), kind=kOutput, calls=%fused_computation.112 | convolution fusion | flops 6444023808 | bytes 22544384 | tf_op jit(solution)/shard_map/dot_general | solution.py:16
  190.4 2.0 reshape.569
  192.4 1.6 fusion.63
  194.0 2.0 reshape.568
  197.0 2.2 fusion.57
  206.1 2.0 copy.47
  208.2 11.3 %fusion.68 = f32[1024,512]{1,0:T(8,128)} fusion(bf16[1024,4096]{1,0:T(8,128)(2,1)} %all-gather.3.cloned.1.call-done, bf16[4096,512]{1,0:T(8,128)(2,1)} %param.25), kind=kOutput, calls=%fused_computation.114 | convolution fusion | flops 4294967296 | bytes 14680064 | tf_op jit(solution)/shard_map/dot_general | solution.py:16
  220.6 4.5 fusion.24
  225.1 1.3 fusion.70
  226.5 2.4 fusion.16
  228.9 8.3 %fusion.69 = f32[1024,4096]{1,0:T(8,128)} fusion(bf16[1024,512]{1,0:T(8,128)(2,1)S(1)} %fusion.24, bf16[512,4096]{1,0:T(8,128)(2,1)S(1)} %copy-done.9), kind=kOutput, calls=%fused_computation.115 | convolution fusion | flops 4294967296 | bytes 22020096 | tf_op jit(solution)/shard_map/dot_general | solution.py:16
  237.2 14.0 %all-gather.5.cloned.1.call-done = bf16[2,8192,256]{1,2,0:T(8,128)(2,1)} async-done(((bf16[2,1024,256]{1,2,0:T(8,128)(2,1)}), bf16[2,8192,256]{1,2,0:T(8,128)(2,1)}) %all-gather.5.cloned.1.call-update) | async-done | bytes 8388624 | tf_op jit(solution)/shard_map/all_gather | solution.py:151
  251.2 49.0 %conditional.1 = (f32[1024,1]{0,1:T(1,128)S(1)}, f32[1024,1,256]{2,0,1:T(8,128)S(1)}) conditional(s32[]{:T(128)} %convert_element_type.83, () %tuple.13, (s32[8192]{0:T(1024)S(1)}, s32[1024]{0:T(1024)S(1)}, s32[8192]{0:T(1024)S(1)}, s32[]{:T(128)}, s32[1024]{0:T(1024)S(1)}, /*index=5*/bf16[2,8192,256]{1,2,0:T(8,128)(2,1)}, ...), branch_computations={%region_9.10_spmd, %region_10.13_spmd} | conditional | flops 8774483968 | bytes 129753136 | solution.py:182
  251.2 12.0 %copy.45 = bf16[2,8192,256]{2,1,0:T(8,128)(2,1)} copy(bf16[2,8192,256]{1,2,0:T(8,128)(2,1)} %get-tuple-element.65) | data formatting | bytes 16777216 | tf_op jit(solution)/shard_map
  263.2 10.0 %fusion = (f32[1024]{0:T(1024)S(1)}, f32[8192,1024]{1,0:T(8,128)S(1)}) fusion(s32[1024]{0:T(1024)S(1)} %broadcast_add_fusion, s32[1024]{0:T(1024)S(1)} %get-tuple-element.22, s32[8192]{0:T(1024)S(1)} %get-tuple-element.23, s32[8192]{0:T(1024)S(1)} %get-tuple-element.21, bf16[1024,1,256]{0,2,1:T(8,128)(2,1)S(1)} %copy-done.4, bf16[2,8192,256]{2,1,0:T(8,128)(2,1)} %copy.45), kind=kOutput, calls=%fused_computation.4 | convolution fusion | flops 4345297920 | bytes 38350848 | tf_op jit(solution)/shard_map/cond/branch_1_fun/qhd,khd->qhk/dot_general | solution.py:164
  273.2 14.2 %fusion.7 = f32[1024,1,256]{2,0,1:T(8,128)S(1)} fusion(bf16[2,8192,256]{2,1,0:T(8,128)(2,1)} %copy.45, f32[8192,1024]{1,0:T(8,128)S(1)} %get-tuple-element.70, f32[1024]{0:T(1024)S(1)} %broadcast_maximum_fusion, s32[1024]{0:T(1024)S(1)} %broadcast_add_fusion, s32[1024]{0:T(1024)S(1)} %get-tuple-element.22, s32[8192]{0:T(1024)S(1)} %get-tuple-element.23, ...), kind=kOutput, calls=%fused_computation.12 | convolution fusion | flops 4362076160 | bytes 38875136 | tf_op jit(solution)/shard_map/cond/branch_1_fun/qhk,khd->qhd/dot_general | solution.py:174
  287.4 12.8 %fusion.2 = f32[1024]{0:T(1024)S(1)} fusion(f32[8192,1024]{1,0:T(8,128)S(1)} %get-tuple-element.70, f32[1024]{0:T(1024)S(1)} %broadcast_maximum_fusion, s32[1024]{0:T(1024)S(1)} %broadcast_add_fusion, s32[1024]{0:T(1024)S(1)} %get-tuple-element.22, s32[8192]{0:T(1024)S(1)} %get-tuple-element.23, s32[8192]{0:T(1024)S(1)} %get-tuple-element.21), kind=kLoop, calls=%fused_computation.6 | loop fusion | flops 67107840 | bytes 33636352 | tf_op jit(solution)/shard_map/cond/branch_1_fun/reduce_sum | solution.py:173
  300.2 1.9 multiply_reduce_fusion
  302.9 8.1 %fusion.25 = f32[1024,4096]{1,0:T(8,128)} fusion(bf16[1,256,4096]{2,1,0:T(8,128)(2,1)S(1)} %copy-done, f32[1024,1,256]{2,0,1:T(8,128)S(1)} %get-tuple-element.30, f32[1024]{0:T(1024)S(1)} %bitcast.116), kind=kOutput, calls=%fused_computation.37 | convolution fusion | flops 2148007936 | bytes 19927040 | tf_op jit(solution)/shard_map/dot_general | solution.py:16
  311.0 73.2 %all-reduce.6.cloned.1.call-done = bf16[1024,32]{0,1:T(8,128)(2,1)} async-done(((bf16[1024,32]{0,1:T(8,128)(2,1)}), bf16[1024,32]{0,1:T(8,128)(2,1)}) %all-reduce.6.cloned.1.call-update) | async-done | bytes 65552 | tf_op jit(solution)/shard_map/psum | solution.py:201
  385.0 15.6 %add_convert_fusion = bf16[1024,4096]{1,0:T(8,128)(2,1)} fusion(f32[1024,4096]{1,0:T(8,128)} %fusion.25, f32[1024,4096]{1,0:T(8,128)} %fusion.69, bf16[1024,128]{0,1:T(8,128)(2,1)S(1)} %bitcast.112, bf16[128,4096]{1,0:T(8,128)(2,1)} %param.34), kind=kOutput, calls=%fused_computation.19 | convolution fusion | flops 1086324736 | bytes 43253760 | tf_op jit(solution)/shard_map/dot_general | solution.py:16
  400.7 84.6 %reduce-scatter.2.cloned.1.call-done = bf16[64,4096]{1,0:T(8,128)(2,1)} async-done(((bf16[1024,4096]{1,0:T(8,128)(2,1)}), bf16[64,4096]{1,0:T(8,128)(2,1)}) %reduce-scatter.2.cloned.1.call-update) | async-done | bytes 524304 | tf_op jit(solution)/shard_map/reduce_scatter | solution.py:203
  485.3 2.0 fusion.40
  (75 shorter events, 15.5 us)
Async XLA Ops:
  6.5 296.3 %copy-start = (bf16[1,256,4096]{2,1,0:T(8,128)(2,1)S(1)}, bf16[1,256,4096]{2,1,0:T(8,128)(2,1)}, u32[]{:S(2)}) copy-start(bf16[1,256,4096]{2,1,0:T(8,128)(2,1)} %param.24) | copy-start | bytes 6291460
  6.5 13.5 %copy-start.8 = (s32[4]{0:T(128)S(1)}, s32[4]{0:T(128)}, u32[]{:S(2)}) copy-start(s32[4]{0:T(128)} %param.37) | copy-start | bytes 52
  6.5 78.4 %copy-start.2 = (bf16[4096,128]{1,0:T(8,128)(2,1)S(1)}, bf16[4096,128]{1,0:T(8,128)(2,1)}, u32[]{:S(2)}) copy-start(bf16[4096,128]{1,0:T(8,128)(2,1)} %param.29) | copy-start | bytes 3145732
  6.5 78.4 %all-gather.3.cloned.1.call-start = ((), (), s32[]{:S(2)}) async-start(), calls=%async_computation.1 | async-start | bytes 8912896 | tf_op jit(solution)/shard_map/all_gather | solution.py:102
  11.4 161.2 %all-reduce.4.cloned.1.call-start = ((), (), s32[]{:S(2)}) async-start(), calls=%async_computation.2 | async-start | bytes 131072 | tf_op jit(solution)/shard_map/psum | solution.py:117
  91.9 159.3 %all-gather.5.cloned.1.call-start = ((), (), s32[]{:S(2)}) async-start(), calls=%async_computation.3 | async-start | bytes 9437184 | tf_op jit(solution)/shard_map/all_gather | solution.py:151
  202.1 182.1 %all-reduce.6.cloned.1.call-start = ((), (), s32[]{:S(2)}) async-start(), calls=%async_computation.4 | async-start | bytes 131072 | tf_op jit(solution)/shard_map/psum | solution.py:201
  208.2 11.3 %copy-start.5 = (bf16[1024,1,32,1]{0,2,3,1:T(8,128)(2,1)S(1)}, bf16[1024,1,32,1]{0,2,3,1:T(8,128)(2,1)}, u32[]{:S(2)}) copy-start(bf16[1024,1,32,1]{0,2,3,1:T(8,128)(2,1)} %get-tuple-element.75) | copy-start | bytes 196612
  208.2 11.3 %copy-start.6 = (bf16[1024,1,32,1]{0,2,3,1:T(8,128)(2,1)S(1)}, bf16[1024,1,32,1]{0,2,3,1:T(8,128)(2,1)}, u32[]{:S(2)}) copy-start(bf16[1024,1,32,1]{0,2,3,1:T(8,128)(2,1)} %get-tuple-element.76) | copy-start | bytes 196612
  208.2 12.4 %copy-start.11 = (f32[512]{0:T(512)S(1)}, f32[512]{0:T(512)}, u32[]{:S(2)}) copy-start(f32[512]{0:T(512)} %param.26) | copy-start | bytes 6148
  220.6 4.6 copy-start.10
  225.1 1.4 copy-start.3
  225.1 3.8 copy-start.9
  251.2 12.0 %copy-start.4 = (bf16[1024,1,256]{0,2,1:T(8,128)(2,1)S(1)}, bf16[1024,1,256]{0,2,1:T(8,128)(2,1)}, u32[]{:S(2)}) copy-start(bf16[1024,1,256]{0,2,1:T(8,128)(2,1)} %get-tuple-element.66) | copy-start | bytes 1572868 | tf_op jit(solution)/shard_map/cond
  302.8 182.5 %reduce-scatter.2.cloned.1.call-start = ((), (), s32[]{:S(2)}) async-start(), calls=%async_computation.5 | async-start | bytes 8912896 | tf_op jit(solution)/shard_map/reduce_scatter | solution.py:203
  400.6 84.7 %copy-start.1 = (bf16[64,4096]{1,0:T(8,128)(2,1)S(1)}, bf16[64,4096]{1,0:T(8,128)(2,1)}, u32[]{:S(2)}) copy-start(bf16[64,4096]{1,0:T(8,128)(2,1)} %param.20) | copy-start | bytes 1572868
  400.6 84.7 %copy-start.7 = (f32[4096]{0:T(1024)S(1)}, f32[4096]{0:T(1024)}, u32[]{:S(2)}) copy-start(f32[4096]{0:T(1024)} %param.28) | copy-start | bytes 49156
Sparse Core Ops, SparseCore 0:
  11.5 73.3 all-gather.2
  92.0 80.5 all-reduce.3
  202.2 48.9 all-gather.4
  302.9 81.1 all-reduce.5
  400.8 84.4 reduce-scatter.1
where the time goes:
time: 495 us; the launch traced here: 494 us
  waiting for transfers between devices  316 us (64%)
  matrix products  95.9 us (19%)
  other arithmetic  34.2 us (7%)
  local copies, waits for them, and re-layouts  32.5 us (7%)
  between operations  14.7 us (3%)
    reduce_scatter x1, waiting for transfers between devices, per_device(): lax.psum_scatter((rank_product(attention_output, output_rows) + (rank_pro...  84.6 us
    psum x1, waiting for transfers between devices, per_device(): rank_input = lax.psum(rank_part.astype(jnp.bfloat16), 'mlp')  80.1 us
    psum x1, waiting for transfers between devices, per_device(): rank_output = lax.psum(rank_part_out.astype(jnp.bfloat16), 'mlp')  73.2 us
    dot_general x10, matrix products, rank_product(): return jnp.dot(left_side, right_side, preferred_element_type=jnp.float32)  71.7 us
    all_gather x1, waiting for transfers between devices, per_device(): slot_portion = lax.all_gather(normed_rows, 'mlp', axis=0, tiled=True)  64.1 us
    dot_general x1, matrix products, attend(): jnp.einsum('qhk,khd->qhd', weights.astype(jnp.bfloat16), part_values, pre...  14.2 us
    all_gather x1, waiting for transfers between devices, per_device(): slot_portion = lax.all_gather(paired, 'req', axis=1, tiled=True)  14 us
    reduce_sum x1, other arithmetic, attend(): new_total = jnp.sum(weights, axis=2)  12.8 us
  transfers between devices with their start and end apart: 5, of which 5 were waited for; matrix products, arithmetic and copies ran while one was open for 10% of the time, Pallas kernels for 0%

commit v1 on v0

--- a/solution.py
+++ b/solution.py
@@ -10,6 +10,17 @@
 ADP_DEV = 4
 EPSILON = 1e-05
 NEGATIVE_FILL = -1e30
+
+
+def turned_line(block, mesh_axis, dim):
+    count = lax.axis_size(mesh_axis)
+    right = [(i, (i + 1) % count) for i in range(count)]
+    parts = [block]
+    for stride in range(1, count):
+        parts = [lax.ppermute(parts[0], mesh_axis, right), *parts]
+    result = jnp.concatenate(parts, axis=dim)
+    shift = (lax.axis_index(mesh_axis) + 1) * parts[-1].shape[dim]
+    return jnp.roll(result, shift, axis=dim)
 
 
 def rank_product(left_side, right_side):
@@ -148,7 +159,7 @@
         jnp.zeros((tok_grp, heads_local), jnp.float32),
         jnp.zeros((tok_grp, heads_local, HEAD_SIZE), jnp.float32),
     )
-    slot_portion = lax.all_gather(paired, "req", axis=1, tiled=True)
+    slot_portion = turned_line(paired, "req", 1)
     offset = jnp.int32(0)
     amount = slot_portion.shape[1]
     key_index, key_request, key_position, key_adapter = token_info(

time: 495 us -> 598 us (1.21)
  waiting for transfers between devices: 316 us -> 369 us
  local copies, waits for them, and re-layouts: 32.5 us -> 73.5 us
  matrix products: 95.9 us -> 102 us
    ppermute x0 -> x7, waiting for transfers between devices: none -> 71.6 us  [turned_line(): parts = [lax.ppermute(parts[0], mesh_axis, right), *parts]]
    unnamed x23 -> x45, local copies, waits for them, and re-layouts: 2.09 us -> 26.7 us
    all_gather x1 -> x0, waiting for transfers between devices: 14 us -> none  [per_device(): slot_portion = lax.all_gather(paired, 'req', axis=1, tiled=True)]
    another operation x2, local copies, waits for them, and re-layouts: 12.1 us -> 21.5 us
  transfers between devices with their start and end apart: 5 -> 11, of which waited for: 5 -> 11; matrix products, arithmetic and copies ran while one was open for 10% -> 9% of each run, Pallas kernels for 0% -> 0%
where the time goes in v1:
time: 598 us; the launch traced here: 597 us
  waiting for transfers between devices  369 us (62%)
  matrix products  102 us (17%)
  local copies, waits for them, and re-layouts  73.5 us (12%)
  other arithmetic  36.8 us (6%)
  between operations  14.7 us (2%)
    reduce_scatter x1, waiting for transfers between devices, per_device(): lax.psum_scatter((rank_product(attention_output, output_rows) + (rank_pro...  84.4 us
    psum x1, waiting for transfers between devices, per_device(): rank_input = lax.psum(rank_part.astype(jnp.bfloat16), 'mlp')  80.1 us
    ppermute x7, waiting for transfers between devices, turned_line(): parts = [lax.ppermute(parts[0], mesh_axis, right), *parts]  71.6 us
    dot_general x10, matrix products, rank_product(): return jnp.dot(left_side, right_side, preferred_element_type=jnp.float32)  70.7 us
    psum x1, waiting for transfers between devices, per_device(): rank_output = lax.psum(rank_part_out.astype(jnp.bfloat16), 'mlp')  69.8 us
    all_gather x1, waiting for transfers between devices, per_device(): slot_portion = lax.all_gather(normed_rows, 'mlp', axis=0, tiled=True)  63.4 us
    unnamed x45, local copies, waits for them, and re-layouts  26.7 us
    another operation x2, local copies, waits for them, and re-layouts  21.5 us
  transfers between devices with their start and end apart: 11, of which 11 were waited for; matrix products, arithmetic and copies ran while one was open for 9% of the time, Pallas kernels for 0%

profile of v1, /device:TPU:0, one launch (start us, length us, event | category | flops | bytes accessed | tf_op | source)
XLA Modules:
  0.0 596.7 jit_solution(13528822115146618277)
XLA Ops:
  13.8 6.2 %gather_fusion = s32[1024]{0:T(1024)S(1)} fusion(s32[257]{0:T(512)} %param.36, s32[1024]{0:T(1024)S(1)} %maximum_clamp_fusion), kind=kCustom, calls=%fused_computation | custom fusion | bytes 12288 | tf_op jit(solution)/shard_map/jit(_take)/gather | solution.py:45
  21.5 63.4 %all-gather.2.cloned.1.call-done = bf16[1024,4096]{1,0:T(8,128)(2,1)} async-done(((bf16[64,4096]{1,0:T(8,128)(2,1)}), bf16[1024,4096]{1,0:T(8,128)(2,1)}) %all-gather.2.cloned.1.call-update) | async-done | bytes 8388624 | tf_op jit(solution)/shard_map/all_gather | solution.py:113
  84.9 6.5 %fusion.69 = f32[1024,128]{0,1:T(8,128)S(1)} fusion(bf16[1024,4096]{1,0:T(8,128)(2,1)} %all-gather.2.cloned.1.call-done, bf16[4096,128]{1,0:T(8,128)(2,1)} %param.29), kind=kOutput, calls=%fused_computation.131 | convolution fusion | flops 1073741824 | bytes 9961472 | tf_op jit(solution)/shard_map/dot_general | solution.py:27
  92.7 80.1 %all-reduce.4.cloned.1.call-done = bf16[1024,32]{0,1:T(8,128)(2,1)} async-done(((bf16[1024,32]{0,1:T(8,128)(2,1)}), bf16[1024,32]{0,1:T(8,128)(2,1)}) %all-reduce.4.cloned.1.call-update) | async-done | bytes 65552 | tf_op jit(solution)/shard_map/psum | solution.py:128
  175.3 3.3 fusion.31
  178.6 11.2 %fusion.68 = (bf16[1024,1,768]{0,2,1:T(8,128)(2,1)S(1)}, f32[1024,1,768]{0,2,1:T(8,128)S(1)}) fusion(f32[1024,768]{0,1:T(8,128)S(1)} %fusion.31, bf16[1024,4096]{1,0:T(8,128)(2,1)} %all-gather.2.cloned.1.call-done, bf16[4096,1,768]{2,0,1:T(8,128)(2,1)} %param.23), kind=kOutput, calls=%fused_computation.130 | convolution fusion | flops 6444023808 | bytes 22544384 | tf_op jit(solution)/shard_map/dot_general | solution.py:27
  201.4 15.4 %collective-permute-done = bf16[2,1024,256]{1,2,0:T(8,128)(2,1)S(1)} collective-permute-done((bf16[2,1024,256]{1,2,0:T(8,128)(2,1)S(1)}, bf16[2,1024,256]{1,2,0:T(8,128)(2,1)S(1)}, u32[]{:S(2)}, u32[]{:S(2)}) %collective-permute-start) | collective-permute-done | bytes 1048608 | tf_op jit(solution)/shard_map/ppermute | solution.py:20
  217.8 15.4 %collective-permute-done.1 = bf16[2,1024,256]{1,2,0:T(8,128)(2,1)S(1)} collective-permute-done((bf16[2,1024,256]{1,2,0:T(8,128)(2,1)S(1)}, bf16[2,1024,256]{1,2,0:T(8,128)(2,1)S(1)}, u32[]{:S(2)}, u32[]{:S(2)}) %collective-permute-start.1) | collective-permute-done | bytes 1048608 | tf_op jit(solution)/shard_map/ppermute | solution.py:20
  234.2 15.5 %collective-permute-done.2 = bf16[2,1024,256]{1,2,0:T(8,128)(2,1)} collective-permute-done((bf16[2,1024,256]{1,2,0:T(8,128)(2,1)S(1)}, bf16[2,1024,256]{1,2,0:T(8,128)(2,1)}, u32[]{:S(2)}, u32[]{:S(2)}) %collective-permute-start.2) | collective-permute-done | bytes 1048608 | tf_op jit(solution)/shard_map/ppermute | solution.py:20
  256.2 9.3 %collective-permute-done.3 = bf16[2,1024,256]{1,2,0:T(8,128)(2,1)} collective-permute-done((bf16[2,1024,256]{1,2,0:T(8,128)(2,1)}, bf16[2,1024,256]{1,2,0:T(8,128)(2,1)}, u32[]{:S(2)}, u32[]{:S(2)}) %collective-permute-start.3) | collective-permute-done | bytes 1048608 | tf_op jit(solution)/shard_map/ppermute | solution.py:20
  265.5 10.4 %fusion.70 = f32[1024,512]{1,0:T(8,128)} fusion(bf16[1024,4096]{1,0:T(8,128)(2,1)} %all-gather.2.cloned.1.call-done, bf16[4096,512]{1,0:T(8,128)(2,1)} %param.25), kind=kOutput, calls=%fused_computation.132 | convolution fusion | flops 4294967296 | bytes 14680064 | tf_op jit(solution)/shard_map/dot_general | solution.py:27
  281.2 4.4 fusion.26
  287.0 2.4 fusion.18
  289.4 7.5 %collective-permute-done.5 = bf16[2,1024,256]{1,2,0:T(8,128)(2,1)S(1)} collective-permute-done((bf16[2,1024,256]{1,2,0:T(8,128)(2,1)}, bf16[2,1024,256]{1,2,0:T(8,128)(2,1)S(1)}, u32[]{:S(2)}, u32[]{:S(2)}) %collective-permute-start.5) | collective-permute-done | bytes 1048608 | tf_op jit(solution)/shard_map/ppermute | solution.py:20
  296.9 8.1 %fusion.71 = f32[1024,4096]{1,0:T(8,128)} fusion(bf16[1024,512]{1,0:T(8,128)(2,1)S(1)} %fusion.26, bf16[512,4096]{1,0:T(8,128)(2,1)S(1)} %copy-done.14), kind=kOutput, calls=%fused_computation.133 | convolution fusion | flops 4294967296 | bytes 22020096 | tf_op jit(solution)/shard_map/dot_general | solution.py:27
  304.9 7.4 %collective-permute-done.6 = bf16[2,1024,256]{1,2,0:T(8,128)(2,1)S(1)} collective-permute-done((bf16[2,1024,256]{1,2,0:T(8,128)(2,1)S(1)}, bf16[2,1024,256]{1,2,0:T(8,128)(2,1)S(1)}, u32[]{:S(2)}, u32[]{:S(2)}) %collective-permute-start.6) | collective-permute-done | bytes 1048608 | tf_op jit(solution)/shard_map/ppermute | solution.py:20
  314.3 2.3 constant_dynamic-update-slice_fusion.13
  316.7 2.3 constant_dynamic-update-slice_fusion.12
  319.0 2.3 constant_dynamic-update-slice_fusion.11
  326.5 2.3 constant_dynamic-update-slice_fusion.5
  328.8 2.3 constant_dynamic-update-slice_fusion.4
  331.0 2.3 constant_dynamic-update-slice_fusion.3
  336.5 70.3 %conditional.1 = (f32[1024,1]{0,1:T(1,128)S(1)}, f32[1024,1,256]{0,2,1:T(8,128)S(1)}) conditional(s32[]{:T(128)} %convert_element_type.86, () %tuple.24, (s32[8192]{0:T(1024)S(1)}, s32[1024]{0:T(1024)S(1)}, s32[8192]{0:T(1024)S(1)}, s32[]{:T(128)}, s32[1024]{0:T(1024)S(1)}, /*index=5*/s32[]{:T(128)}, s32[]{:T(128)}, ...), branch_computations={%region_9.10_spmd, %region_10.13_spmd.clone} | conditional | flops 8774483968 | bytes 280748288 | solution.py:193
  336.6 21.4 %copy.49 = bf16[2,16384,256]{2,1,0:T(8,128)(2,1)} copy(bf16[2,16384,256]{1,2,0:T(8,128)(2,1)} %get-tuple-element.216) | data formatting | bytes 33554432 | tf_op jit(solution)/shard_map
  358.0 14.7 %fusion = (f32[1024]{0:T(1024)S(1)}, f32[8192,1024]{1,0:T(8,128)}) fusion(s32[1024]{0:T(1024)S(1)} %broadcast_add_fusion, s32[1024]{0:T(1024)S(1)} %get-tuple-element.144, s32[8192]{0:T(1024)S(1)} %get-tuple-element.145, s32[8192]{0:T(1024)S(1)} %get-tuple-element.143, bf16[1024,1,256]{0,2,1:T(8,128)(2,1)S(1)} %copy-done.8, ...), kind=kOutput, calls=%fused_computation.4 | convolution fusion | flops 4345297920 | bytes 38350852 | tf_op jit(solution)/shard_map/cond/branch_1_fun/qhd,khd->qhk/dot_general | solution.py:175
  372.7 16.6 %fusion.7 = f32[1024,1,256]{0,2,1:T(8,128)S(1)} fusion(f32[8192,1024]{1,0:T(8,128)} %get-tuple-element.225, f32[1024]{0:T(1024)S(1)} %broadcast_maximum_fusion, s32[1024]{0:T(1024)S(1)} %broadcast_add_fusion, s32[1024]{0:T(1024)S(1)} %get-tuple-element.144, s32[8192]{0:T(1024)S(1)} %get-tuple-element.145, s32[8192]{0:T(1024)S(1)} %get-tuple-element.143, ...), kind=kOutput, calls=%fused_computation.12 | convolution fusion | flops 4362076160 | bytes 38875144 | tf_op jit(solution)/shard_map/cond/branch_1_fun/qhk,khd->qhd/dot_general | solution.py:185
  389.3 4.8 copy-done.1
  394.1 12.7 %fusion.2 = f32[1024]{0:T(1024)S(1)} fusion(f32[8192,1024]{1,0:T(8,128)S(1)} %copy-done.1, f32[1024]{0:T(1024)S(1)} %broadcast_maximum_fusion, s32[1024]{0:T(1024)S(1)} %broadcast_add_fusion, s32[1024]{0:T(1024)S(1)} %get-tuple-element.144, s32[8192]{0:T(1024)S(1)} %get-tuple-element.145, s32[8192]{0:T(1024)S(1)} %get-tuple-element.143), kind=kLoop, calls=%fused_computation.6 | loop fusion | flops 67107840 | bytes 33636352 | tf_op jit(solution)/shard_map/cond/branch_1_fun/reduce_sum | solution.py:184
  409.3 8.1 %fusion.27 = f32[1024,4096]{1,0:T(8,128)} fusion(bf16[1,256,4096]{2,1,0:T(8,128)(2,1)S(1)} %copy-done, f32[1024,1,256]{0,2,1:T(8,128)S(1)} %get-tuple-element.135, f32[1024]{0:T(1024)S(1)} %bitcast.115), kind=kOutput, calls=%fused_computation.39 | convolution fusion | flops 2148007936 | bytes 19927040 | tf_op jit(solution)/shard_map/dot_general | solution.py:27
  417.5 69.8 %all-reduce.6.cloned.1.call-done = bf16[1024,32]{0,1:T(8,128)(2,1)} async-done(((bf16[1024,32]{0,1:T(8,128)(2,1)}), bf16[1024,32]{0,1:T(8,128)(2,1)}) %all-reduce.6.cloned.1.call-update) | async-done | bytes 65552 | tf_op jit(solution)/shard_map/psum | solution.py:212
  488.1 15.6 %add_convert_fusion = bf16[1024,4096]{1,0:T(8,128)(2,1)} fusion(f32[1024,4096]{1,0:T(8,128)} %fusion.27, f32[1024,4096]{1,0:T(8,128)} %fusion.71, bf16[1024,128]{0,1:T(8,128)(2,1)S(1)} %bitcast.111, bf16[128,4096]{1,0:T(8,128)(2,1)} %param.34), kind=kOutput, calls=%fused_computation.21 | convolution fusion | flops 1086324736 | bytes 43253760 | tf_op jit(solution)/shard_map/dot_general | solution.py:27
  503.8 84.4 %reduce-scatter.2.cloned.1.call-done = bf16[64,4096]{1,0:T(8,128)(2,1)} async-done(((bf16[1024,4096]{1,0:T(8,128)(2,1)}), bf16[64,4096]{1,0:T(8,128)(2,1)}) %reduce-scatter.2.cloned.1.call-update) | async-done | bytes 524304 | tf_op jit(solution)/shard_map/reduce_scatter | solution.py:214
  (112 shorter events, 53.6 us)
Async XLA Ops:
  6.5 402.8 %copy-start = (bf16[1,256,4096]{2,1,0:T(8,128)(2,1)S(1)}, bf16[1,256,4096]{2,1,0:T(8,128)(2,1)}, u32[]{:S(2)}) copy-start(bf16[1,256,4096]{2,1,0:T(8,128)(2,1)} %param.24) | copy-start | bytes 6291460
  6.5 78.4 %all-gather.2.cloned.1.call-start = ((), (), s32[]{:S(2)}) async-start(), calls=%async_computation.1 | async-start | bytes 8912896 | tf_op jit(solution)/shard_map/all_gather | solution.py:113
  11.4 161.4 %all-reduce.4.cloned.1.call-start = ((), (), s32[]{:S(2)}) async-start(), calls=%async_computation.2 | async-start | bytes 131072 | tf_op jit(solution)/shard_map/psum | solution.py:128
  92.1 395.1 %all-reduce.6.cloned.1.call-start = ((), (), s32[]{:S(2)}) async-start(), calls=%async_computation.3 | async-start | bytes 131072 | tf_op jit(solution)/shard_map/psum | solution.py:212
  201.3 15.4 %collective-permute-start = (bf16[2,1024,256]{1,2,0:T(8,128)(2,1)S(1)}, bf16[2,1024,256]{1,2,0:T(8,128)(2,1)S(1)}, u32[]{:S(2)}, u32[]{:S(2)}) collective-permute-start(bf16[2,1024,256]{1,2,0:T(8,128)(2,1)S(1)} %pad_maximum_fusion), channel_id=1, source_target_pairs={{0,16},{16,32},{32,48},{48,64},{64,80},{80,96},{96,112},{112,0},{1... | collective-permute-start | bytes 3145736 | tf_op jit(solution)/shard_map/ppermute | solution.py:20
  216.8 1.0 copy-start.3
  217.8 15.4 %collective-permute-start.1 = (bf16[2,1024,256]{1,2,0:T(8,128)(2,1)S(1)}, bf16[2,1024,256]{1,2,0:T(8,128)(2,1)S(1)}, u32[]{:S(2)}, u32[]{:S(2)}) collective-permute-start(bf16[2,1024,256]{1,2,0:T(8,128)(2,1)S(1)} %collective-permute-done), channel_id=1, source_target_pairs={{0,16},{16,32},{32,48},{48,64},{64,80},{80,96},{96,112},{112,0},{1... | collective-permute-start | bytes 3145736 | tf_op jit(solution)/shard_map/ppermute | solution.py:20
  233.2 1.0 copy-start.5
  234.2 15.5 %collective-permute-start.2 = (bf16[2,1024,256]{1,2,0:T(8,128)(2,1)S(1)}, bf16[2,1024,256]{1,2,0:T(8,128)(2,1)}, u32[]{:S(2)}, u32[]{:S(2)}) collective-permute-start(bf16[2,1024,256]{1,2,0:T(8,128)(2,1)S(1)} %collective-permute-done.1), channel_id=1, source_target_pairs={{0,16},{16,32},{32,48},{48,64},{64,80},{80,96},{96,112},{112,0},{1... | collective-permute-start | bytes 3145736 | tf_op jit(solution)/shard_map/ppermute | solution.py:20
  249.7 15.8 %collective-permute-start.3 = (bf16[2,1024,256]{1,2,0:T(8,128)(2,1)}, bf16[2,1024,256]{1,2,0:T(8,128)(2,1)}, u32[]{:S(2)}, u32[]{:S(2)}) collective-permute-start(bf16[2,1024,256]{1,2,0:T(8,128)(2,1)} %collective-permute-done.2), channel_id=1, source_target_pairs={{0,16},{16,32},{32,48},{48,64},{64,80},{80,96},{96,112},{112,0},{1... | collective-permute-start | bytes 3145736 | tf_op jit(solution)/shard_map/ppermute | solution.py:20
  251.6 0.6 copy-start.11
  256.2 19.6 %copy-start.9 = (bf16[1024,1,32,1]{0,2,3,1:T(8,128)(2,1)S(1)}, bf16[1024,1,32,1]{0,2,3,1:T(8,128)(2,1)}, u32[]{:S(2)}) copy-start(bf16[1024,1,32,1]{0,2,3,1:T(8,128)(2,1)} %get-tuple-element.230) | copy-start | bytes 196612
  256.2 19.6 %copy-start.10 = (bf16[1024,1,32,1]{0,2,3,1:T(8,128)(2,1)S(1)}, bf16[1024,1,32,1]{0,2,3,1:T(8,128)(2,1)}, u32[]{:S(2)}) copy-start(bf16[1024,1,32,1]{0,2,3,1:T(8,128)(2,1)} %get-tuple-element.231) | copy-start | bytes 196612
  256.2 25.0 %copy-start.16 = (f32[512]{0:T(512)S(1)}, f32[512]{0:T(512)}, u32[]{:S(2)}) copy-start(f32[512]{0:T(512)} %param.26) | copy-start | bytes 6148
  265.5 15.8 %collective-permute-start.4 = (bf16[2,1024,256]{1,2,0:T(8,128)(2,1)}, bf16[2,1024,256]{1,2,0:T(8,128)(2,1)}, u32[]{:S(2)}, u32[]{:S(2)}) collective-permute-start(bf16[2,1024,256]{1,2,0:T(8,128)(2,1)} %collective-permute-done.3), channel_id=1, source_target_pairs={{0,16},{16,32},{32,48},{48,64},{64,80},{80,96},{96,112},{112,0},{1... | collective-permute-start | bytes 3145736 | tf_op jit(solution)/shard_map/ppermute | solution.py:20
  278.2 7.4 %copy-start.15 = (bf16[512,1024]{1,0:T(8,128)(2,1)S(1)}, bf16[512,1024]{1,0:T(8,128)(2,1)}, u32[]{:S(2)}) copy-start(bf16[512,1024]{1,0:T(8,128)(2,1)} %param.33) | copy-start | bytes 3145732
  281.2 15.6 %collective-permute-start.5 = (bf16[2,1024,256]{1,2,0:T(8,128)(2,1)}, bf16[2,1024,256]{1,2,0:T(8,128)(2,1)S(1)}, u32[]{:S(2)}, u32[]{:S(2)}) collective-permute-start(bf16[2,1024,256]{1,2,0:T(8,128)(2,1)} %collective-permute-done.4), channel_id=1, source_target_pairs={{0,16},{16,32},{32,48},{48,64},{64,80},{80,96},{96,112},{112,0},{1... | collective-permute-start | bytes 3145736 | tf_op jit(solution)/shard_map/ppermute | solution.py:20
  281.2 5.8 copy-start.7
  285.6 11.2 %copy-start.14 = (bf16[512,4096]{1,0:T(8,128)(2,1)S(1)}, bf16[512,4096]{1,0:T(8,128)(2,1)}, u32[]{:S(2)}) copy-start(bf16[512,4096]{1,0:T(8,128)(2,1)} %param.27) | copy-start | bytes 12582916
  296.9 15.4 %collective-permute-start.6 = (bf16[2,1024,256]{1,2,0:T(8,128)(2,1)S(1)}, bf16[2,1024,256]{1,2,0:T(8,128)(2,1)S(1)}, u32[]{:S(2)}, u32[]{:S(2)}) collective-permute-start(bf16[2,1024,256]{1,2,0:T(8,128)(2,1)S(1)} %collective-permute-done.5), channel_id=1, source_target_pairs={{0,16},{16,32},{32,48},{48,64},{64,80},{80,96},{96,112},{112,0},{1... | collective-permute-start | bytes 3145736 | tf_op jit(solution)/shard_map/ppermute | solution.py:20
  304.9 16.3 %copy-start.6 = (bf16[2,1024,256]{1,2,0:T(8,128)(2,1)S(1)}, bf16[2,1024,256]{1,2,0:T(8,128)(2,1)}, u32[]{:S(2)}) copy-start(bf16[2,1024,256]{1,2,0:T(8,128)(2,1)} %copy-done.5) | copy-start | bytes 3145732
  304.9 17.3 %copy-start.4 = (bf16[2,1024,256]{1,2,0:T(8,128)(2,1)S(1)}, bf16[2,1024,256]{1,2,0:T(8,128)(2,1)}, u32[]{:S(2)}) copy-start(bf16[2,1024,256]{1,2,0:T(8,128)(2,1)} %copy-done.3) | copy-start | bytes 3145732
  324.4 12.1 %copy-start.12 = (s32[8192]{0:T(1024)S(1)}, s32[8192]{0:T(1024)}, u32[]{:S(2)}) copy-start(s32[8192]{0:T(1024)} %copy-done.11) | copy-start | bytes 98308
  336.6 21.4 %copy-start.8 = (bf16[1024,1,256]{0,2,1:T(8,128)(2,1)S(1)}, bf16[1024,1,256]{0,2,1:T(8,128)(2,1)}, u32[]{:S(2)}) copy-start(bf16[1024,1,256]{0,2,1:T(8,128)(2,1)} %get-tuple-element.217) | copy-start | bytes 1572868 | tf_op jit(solution)/shard_map/cond
  372.7 21.4 %copy-start.1 = (f32[8192,1024]{1,0:T(8,128)S(1)}, f32[8192,1024]{1,0:T(8,128)}, u32[]{:S(2)}) copy-start(f32[8192,1024]{1,0:T(8,128)} %get-tuple-element.225) | copy-start | bytes 100663296 | tf_op jit(solution)/shard_map/cond
  409.3 178.9 %reduce-scatter.2.cloned.1.call-start = ((), (), s32[]{:S(2)}) async-start(), calls=%async_computation.4 | async-start | bytes 8912896 | tf_op jit(solution)/shard_map/reduce_scatter | solution.py:214
  503.8 84.5 %copy-start.2 = (bf16[64,4096]{1,0:T(8,128)(2,1)S(1)}, bf16[64,4096]{1,0:T(8,128)(2,1)}, u32[]{:S(2)}) copy-start(bf16[64,4096]{1,0:T(8,128)(2,1)} %param.20) | copy-start | bytes 1572868
  503.8 84.5 %copy-start.13 = (f32[4096]{0:T(1024)S(1)}, f32[4096]{0:T(1024)}, u32[]{:S(2)}) copy-start(f32[4096]{0:T(1024)} %param.28) | copy-start | bytes 49156
Sparse Core Ops, SparseCore 0:
  11.5 73.3 all-gather.1
  92.2 80.5 all-reduce.3
  409.4 77.8 all-reduce.5
  503.9 84.2 reduce-scatter.1
